TPU v7x, 128 devices: a whole 4x4x4 slice. The times are simulated.
128 devices in a mesh: tile: 64 (over z, y, x), slide: 2 (over core).
Axes of the slice: x: 4, y: 4, z: 4, core: 2. Of those that a mesh axis runs over, the one named last changes fastest.
Arguments:
- features: bfloat16 [256, 32, 32, 256], P(('slide', 'tile')), parts along dimension 0, may hold values from -8 to 8
- neighbours: int32 [256, 8], P(('slide', 'tile')), parts along dimension 0, may hold values from 0 to 128, as said below
- conv_weight: bfloat16 [3, 3, 256, 256], replicated, may hold values from -0.125 to 0.125
- patch_weight: bfloat16 [4096, 768], replicated, may hold values from -1 to 1
- query_weight: bfloat16 [768, 768], replicated, may hold values from -2 to 2
- key_weight: bfloat16 [768, 768], replicated, may hold values from -2 to 2
- value_weight: bfloat16 [768, 768], replicated, may hold values from -0.21875 to 0.21875
- output_weight: bfloat16 [768, 768], replicated, may hold values from -0.21875 to 0.21875
- cotangent: bfloat16 [16384, 768], P(('slide', 'tile')), parts along dimension 0, may hold values from -6 to 6
Outputs:
- mixed: bfloat16 [16384, 768], P(('slide', 'tile')), parts along dimension 0
- output_grad: float32 [1536, 768], P('slide'), parts along dimension 0
There are 2 independent parts, one for each index of `slide`. A program takes and returns all parts, laid end to end along the dimension named above; an argument that names none is the same for every part. Nothing has to cross between parts.
Inputs may be any that keep to these rules, and one draw needn't show every extreme that they name: Tiles are tissue cells of a grid 16 cells wide; the tile numbers are given to the tissue cells in a drawn order, so neighbours may have any numbers; each entry is the index of the tissue tile at that grid offset, or 128.
All inputs are finite; a program needn't handle non-finite values.
Results may differ from a plain program's by a relative error of at most 0.02.
Values may be sent and summed in bfloat16 or wider, within the bound.
No kernel may reach another device: no remote copies, remote signals or barrier semaphores. Data moves between devices by JAX's collectives and lax.ppermute only.
A program may use at most 192 MiB of HBM per device.

v0:
```python
import jax
import jax.numpy as jnp
from jax import lax
from jax.sharding import PartitionSpec as P

PATCH = 4
HEADS = 12
HD = 64


def tile_faces(maps):
    return jnp.stack([maps[:, 0], maps[:, -1], maps[:, :, 0], maps[:, :, -1]], axis=1)


def pad_tiles(maps, all_faces, links):
    upper = all_faces[links[:, 1], 1]
    lower = all_faces[links[:, 6], 0]
    left_col = all_faces[links[:, 3], 3]
    right_col = all_faces[links[:, 4], 2]
    corner_ul = all_faces[links[:, 0], 1, -1]
    corner_ur = all_faces[links[:, 2], 1, 0]
    corner_dl = all_faces[links[:, 5], 0, -1]
    corner_dr = all_faces[links[:, 7], 0, 0]
    top_row = jnp.concatenate([corner_ul[:, None], upper, corner_ur[:, None]], axis=1)
    bottom_row = jnp.concatenate([corner_dl[:, None], lower, corner_dr[:, None]], axis=1)
    middle = jnp.concatenate([left_col[:, :, None], maps, right_col[:, :, None]], axis=2)
    return jnp.concatenate([top_row[:, None], middle, bottom_row[:, None]], axis=1)


def conv_tiles(padded, kernel):
    count = padded.shape[0]
    side = padded.shape[1] - 2
    chans = padded.shape[3]
    total = jnp.zeros((count * side * side, kernel.shape[3]), jnp.float32)
    for row_off in range(3):
        for col_off in range(3):
            window = padded[:, row_off : row_off + side, col_off : col_off + side, :].reshape(
                -1, chans
            )
            total = total + jnp.dot(
                window, kernel[row_off, col_off], preferred_element_type=jnp.float32
            )
    return jax.nn.gelu(total).astype(jnp.bfloat16).reshape(count, side, side, -1)


def patchify(hidden, patch):
    count, side, _, chans = hidden.shape
    blocks = side // patch
    grid = hidden.reshape(count, blocks, patch, blocks, patch, chans).transpose(0, 1, 3, 2, 4, 5)
    return grid.reshape(count * blocks * blocks, patch * patch * chans)


def local(
    features,
    neighbours,
    conv_weight,
    patch_weight,
    query_weight,
    key_weight,
    value_weight,
    output_weight,
    cotangent,
):
    local_faces = tile_faces(features)
    gathered = lax.all_gather(local_faces, "tile", axis=0, tiled=True)
    all_faces = jnp.concatenate(
        [gathered, jnp.zeros((1,) + gathered.shape[1:], jnp.bfloat16)], axis=0
    )
    padded = pad_tiles(features, all_faces, neighbours)
    hidden = conv_tiles(padded, conv_weight)
    tokens = jnp.dot(
        patchify(hidden, PATCH), patch_weight, preferred_element_type=jnp.float32
    ).astype(jnp.bfloat16)
    rows = tokens.shape[0]
    query = (
        jnp.dot(tokens, query_weight, preferred_element_type=jnp.float32)
        .astype(jnp.bfloat16)
        .reshape(rows, HEADS, HD)
    )
    scale = HD ** (-0.5)
    keys = jnp.dot(tokens, key_weight, preferred_element_type=jnp.float32).astype(jnp.bfloat16)
    values = jnp.dot(tokens, value_weight, preferred_element_type=jnp.float32).astype(jnp.bfloat16)
    top = jnp.full((HEADS, rows), -1e30, jnp.float32)
    key_heads = lax.all_gather(keys, "tile", axis=0, tiled=True).reshape(-1, HEADS, HD)
    value_heads = lax.all_gather(values, "tile", axis=0, tiled=True).reshape(-1, HEADS, HD)
    scores = (
        jnp.einsum("qhd,khd->hqk", query, key_heads, preferred_element_type=jnp.float32) * scale
    )
    new_top = jnp.maximum(top, jnp.max(scores, axis=-1))
    weights = jnp.exp(scores - new_top[..., None])
    total = jnp.sum(weights, axis=-1)
    accum = jnp.einsum(
        "hqk,khd->hqd",
        weights.astype(jnp.bfloat16),
        value_heads,
        preferred_element_type=jnp.float32,
    )
    top, total, accum = (new_top, total, accum)
    attended = (
        (accum / total[..., None]).transpose(1, 0, 2).reshape(rows, HEADS * HD).astype(jnp.bfloat16)
    )
    mixed = (
        tokens.astype(jnp.float32)
        + jnp.dot(attended, output_weight, preferred_element_type=jnp.float32)
    ).astype(jnp.bfloat16)
    grad_term = jnp.dot(attended.T, cotangent, preferred_element_type=jnp.float32)
    output_grad = lax.psum(grad_term, "tile")
    return (mixed, output_grad)


def solution(mesh):
    in_specs = (
        P(("slide", "tile"), None, None, None),
        P(("slide", "tile"), None),
        P(),
        P(),
        P(),
        P(),
        P(),
        P(),
        P(("slide", "tile"), None),
    )
    out_specs = (P(("slide", "tile"), None), P("slide", None))
    return jax.shard_map(local, mesh=mesh, in_specs=in_specs, out_specs=out_specs, check_vma=False)
```

profile of v0, /device:TPU:0, one launch (start us, length us, event | category | flops | bytes accessed | tf_op | source)
XLA Modules:
  0.0 506.7 jit_solution(2070060483644725372)
XLA Ops:
  7.2 1.2 fusion.78
  8.5 0.8 fusion.77
  9.3 0.7 pad_maximum_fusion.3
  10.0 1.3 fusion.68
  11.3 81.0 %all-gather.4.cloned.1.call-done = bf16[128,4,32,256]{3,2,1,0:T(8,128)(2,1)} async-done(((bf16[2,4,32,256]{3,2,1,0:T(8,128)(2,1)}), bf16[128,4,32,256]{3,2,1,0:T(8,128)(2,1)}) %all-gather.4.cloned.1.call-update) | async-done | bytes 8388624 | tf_op jit(solution)/shard_map/all_gather | solution.py:65
  92.3 8.5 %concatenate.53 = bf16[129,4,32,256]{3,2,1,0:T(8,128)(2,1)} pad(bf16[128,4,32,256]{3,2,1,0:T(8,128)(2,1)} %all-gather.4.cloned.1.call-done, bf16[]{:T(256)} %constant.15.clone.1), padding=0_1x0_0x0_0x0_0 | pad | bytes 16842754 | tf_op jit(solution)/shard_map/concatenate | solution.py:66
  100.8 3.9 gather_fusion.1
  104.8 1.5 gather_fusion
  106.3 1.5 gather_fusion.2
  107.8 3.9 gather_fusion.6
  111.7 1.5 gather_fusion.5
  113.2 1.5 gather_fusion.7
  114.7 3.9 gather_fusion.3
  118.7 4.0 gather_fusion.4
  122.7 1.2 pad_maximum_fusion.1
  124.0 1.7 pad_maximum_fusion
  125.7 0.8 fusion.76
  126.5 0.8 fusion.75
  127.2 0.5 copy-done.5
  127.7 0.4 fusion.32
  128.2 0.4 convolution_add_fusion.7
  128.6 0.4 convolution_add_fusion.6
  129.1 0.4 convolution_add_fusion.5
  129.5 0.4 convolution_add_fusion.4
  129.9 0.4 convolution_add_fusion.3
  130.4 0.4 convolution_add_fusion.2
  130.8 0.5 convolution_add_fusion.1
  131.3 0.9 fusion.13
  132.2 0.3 reshape_reshape.3
  132.5 0.4 copy.60
  132.9 0.8 reshape.58
  133.7 3.8 convolution_convert_fusion.3
  137.5 1.0 convolution_convert_fusion.1
  138.6 2.3 convolution_convert_fusion
  140.9 0.2 all-reduce.8.cloned.1.call-start
  141.2 0.3 convolution_convert_fusion.2
  141.5 0.2 copy.52
  141.7 87.6 %all-gather.6.cloned.1.call-done = bf16[8192,768]{1,0:T(8,128)(2,1)} async-done(((bf16[128,768]{1,0:T(8,128)(2,1)}), bf16[8192,768]{1,0:T(8,128)(2,1)}) %all-gather.6.cloned.1.call-update) | async-done | bytes 12582928 | tf_op jit(solution)/shard_map/all_gather | solution.py:84
  229.2 15.8 %copy.53 = bf16[8192,768]{0,1:T(8,128)(2,1)} copy(bf16[8192,768]{1,0:T(8,128)(2,1)} %all-gather.6.cloned.1.call-done) | data formatting | bytes 25165824 | tf_op jit(solution)/shard_map/all_gather | solution.py:84
  245.0 22.0 %multiply_reduce_fusion = (f32[12,128]{1,0:T(8,128)S(1)}, f32[12,128,8192]{2,1,0:T(8,128)}) fusion(bf16[128,12,64]{0,2,1:T(8,128)(2,1)S(1)} %bitcast.106, bf16[8192,12,64]{0,2,1:T(8,128)(2,1)} %bitcast.92), kind=kOutput, calls=%fused_computation.9 | convolution fusion | flops 1635777024 | bytes 63117312 | tf_op jit(solution)/shard_map/qhd,khd->hqk/dot_general | solution.py:87
  267.0 21.7 %fusion = f32[12,128]{1,0:T(8,128)S(1)} fusion(f32[12,128,8192]{2,1,0:T(8,128)} %get-tuple-element.25, f32[12,128]{1,0:T(8,128)S(1)} %broadcast_maximum_fusion), kind=kLoop, calls=%fused_computation.10 | loop fusion | flops 37747200 | bytes 50343936 | tf_op jit(solution)/shard_map/reduce_sum | solution.py:91
  288.8 34.3 %all-gather.8.cloned.1.call-done = bf16[8192,768]{1,0:T(8,128)(2,1)} async-done(((bf16[128,768]{1,0:T(8,128)(2,1)}), bf16[8192,768]{1,0:T(8,128)(2,1)}) %all-gather.8.cloned.1.call-update) | async-done | bytes 12582928 | tf_op jit(solution)/shard_map/all_gather | solution.py:85
  323.1 15.8 %copy.54 = bf16[8192,768]{0,1:T(8,128)(2,1)} copy(bf16[8192,768]{1,0:T(8,128)(2,1)} %all-gather.8.cloned.1.call-done) | data formatting | bytes 25165824 | tf_op jit(solution)/shard_map/all_gather | solution.py:85
  338.9 22.2 %fusion.21 = bf16[128,12,64]{0,2,1:T(8,128)(2,1)S(1)} fusion(bf16[8192,12,64]{0,2,1:T(8,128)(2,1)} %bitcast.93, f32[12,128,8192]{2,1,0:T(8,128)} %get-tuple-element.25, f32[12,128]{1,0:T(8,128)S(1)} %broadcast_maximum_fusion, f32[128,12]{0,1:T(8,128)S(1)} %bitcast.109), kind=kOutput, calls=%fused_computation.42 | convolution fusion | flops 1648558080 | bytes 63123456 | tf_op jit(solution)/shard_map/hqk,khd->hqd/dot_general | solution.py:92
  361.1 1.9 fusion.79
  363.0 1.0 fusion.17
  364.1 132.8 %all-reduce.8.cloned.1.call-done = f32[768,768]{1,0:T(8,128)} async-done(((f32[768,768]{1,0:T(8,128)}), f32[768,768]{1,0:T(8,128)}) %all-reduce.8.cloned.1.call-update) | async-done | bytes 2359312 | tf_op jit(solution)/shard_map/psum | solution.py:107
  496.9 3.2 copy.62
  (30 shorter events, 0.4 us)
Async XLA Ops:
  7.2 130.3 %copy-start = (bf16[768,768]{1,0:T(8,128)(2,1)S(1)}, bf16[768,768]{1,0:T(8,128)(2,1)}, u32[]{:S(2)}) copy-start(bf16[768,768]{1,0:T(8,128)(2,1)} %param.14) | copy-start | bytes 3538948
  7.2 85.1 %all-gather.4.cloned.1.call-start = ((), (), s32[]{:S(2)}) async-start(), calls=%async_computation | async-start | bytes 8519680 | tf_op jit(solution)/shard_map/all_gather | solution.py:65
  10.0 219.3 %all-gather.6.cloned.1.call-start = ((), (), s32[]{:S(2)}) async-start(), calls=%async_computation.1 | async-start | bytes 12779520 | tf_op jit(solution)/shard_map/all_gather | solution.py:84
  11.3 111.4 %copy-start.2 = (bf16[2,32,32,256]{3,2,1,0:T(8,128)(2,1)S(1)}, bf16[2,32,32,256]{3,2,1,0:T(8,128)(2,1)}, u32[]{:S(2)}) copy-start(bf16[2,32,32,256]{3,2,1,0:T(8,128)(2,1)} %param.9) | copy-start | bytes 3145732
  126.5 1.3 copy-start.5
  137.5 3.6 copy-start.3
  138.6 184.5 %all-gather.8.cloned.1.call-start = ((), (), s32[]{:S(2)}) async-start(), calls=%async_computation.2 | async-start | bytes 12779520 | tf_op jit(solution)/shard_map/all_gather | solution.py:85
  140.9 356.0 %all-reduce.8.cloned.1.call-start = ((), (), s32[]{:S(2)}) async-start(), calls=%async_computation.3 | async-start | bytes 4718592 | tf_op jit(solution)/shard_map/psum | solution.py:107
  338.9 22.2 %copy-start.6 = (bf16[128,768]{1,0:T(8,128)(2,1)S(1)}, bf16[128,768]{1,0:T(8,128)(2,1)}, u32[]{:S(2)}) copy-start(bf16[128,768]{1,0:T(8,128)(2,1)} %param.17) | copy-start | bytes 589828
  361.1 1.9 copy-start.4
  363.0 137.1 %copy-start.1 = (bf16[768,768]{1,0:T(8,128)(2,1)S(1)}, bf16[768,768]{1,0:T(8,128)(2,1)}, u32[]{:S(2)}) copy-start(bf16[768,768]{1,0:T(8,128)(2,1)} %param.14) | copy-start | bytes 3538948
Sparse Core Ops, SparseCore 0:
  11.4 80.8 all-gather.3
  138.7 90.4 all-gather.5
  232.5 90.5 all-gather.7
  363.1 133.7 all-reduce.7
where the time goes:
time: 508 us; the launch traced here: 507 us
  waiting for transfers between devices  336 us (66%)
  local copies, waits for them, and re-layouts  70.9 us (14%)
  matrix products  58.9 us (12%)
  other arithmetic  26.6 us (5%)
  between operations  14 us (3%)
    psum x1, waiting for transfers between devices, local(): output_grad = lax.psum(grad_term, 'tile')  133 us
    all_gather x1, waiting for transfers between devices, local(): lax.all_gather(keys, 'tile', axis=0, tiled=True).reshape(-1, HEADS, HD)  87.6 us
    all_gather x1, waiting for transfers between devices, local(): gathered = lax.all_gather(local_faces, 'tile', axis=0, tiled=True)  81 us
    all_gather x1, waiting for transfers between devices, local(): lax.all_gather(values, 'tile', axis=0, tiled=True).reshape(-1, HEADS, HD)  34.3 us
    dot_general x1, matrix products, local(): jnp.einsum('hqk,khd->hqd', weights.astype(jnp.bfloat16), value_heads, pre...  22.2 us
    dot_general x1, matrix products, local(): jnp.einsum('qhd,khd->hqk', query, key_heads, preferred_element_type=jnp.f...  22 us
    reduce_sum x1, other arithmetic, local(): total = jnp.sum(weights, axis=-1)  21.7 us
    all_gather x1, local copies, waits for them, and re-layouts, local(): lax.all_gather(keys, 'tile', axis=0, tiled=True).reshape(-1, HEADS, HD)  15.8 us
  transfers between devices with their start and end apart: 4, of which 4 were waited for; matrix products, arithmetic and copies ran while one was open for 13% of the time, Pallas kernels for 0%

commit v1 on v0

--- a/solution.py
+++ b/solution.py
@@ -104,7 +104,7 @@
         + jnp.dot(attended, output_weight, preferred_element_type=jnp.float32)
     ).astype(jnp.bfloat16)
     grad_term = jnp.dot(attended.T, cotangent, preferred_element_type=jnp.float32)
-    output_grad = lax.psum(grad_term, "tile")
+    output_grad = jnp.sum(lax.all_gather(grad_term, "tile"), axis=0)
     return (mixed, output_grad)
 
 

time: 508 us -> 990 us (1.95)
  waiting for transfers between devices: 336 us -> 774 us
  other arithmetic: 26.6 us -> 73.6 us
    all_gather x0 -> x1, waiting for transfers between devices: none -> 571 us  [local(): output_grad = jnp.sum(lax.all_gather(grad_term, 'tile'), axis=0)]
    psum x1 -> x0, waiting for transfers between devices: 133 us -> none  [local(): output_grad = lax.psum(grad_term, 'tile')]
    reduce_sum x0 -> x1, other arithmetic: none -> 47 us  [local(): output_grad = jnp.sum(lax.all_gather(grad_term, 'tile'), axis=0)]
  transfers between devices with their start and end apart: 4 -> 4, of which waited for: 4 -> 4; matrix products, arithmetic and copies ran while one was open for 13% -> 7% of each run, Pallas kernels for 0% -> 0%
where the time goes in v1:
time: 990 us; the launch traced here: 988 us
  waiting for transfers between devices  774 us (78%)
  other arithmetic  73.6 us (7%)
  local copies, waits for them, and re-layouts  67.7 us (7%)
  matrix products  58.9 us (6%)
  between operations  14.1 us (1%)
    all_gather x1, waiting for transfers between devices, local(): output_grad = jnp.sum(lax.all_gather(grad_term, 'tile'), axis=0)  571 us
    all_gather x1, waiting for transfers between devices, local(): lax.all_gather(keys, 'tile', axis=0, tiled=True).reshape(-1, HEADS, HD)  87.5 us
    all_gather x1, waiting for transfers between devices, local(): gathered = lax.all_gather(local_faces, 'tile', axis=0, tiled=True)  81 us
    reduce_sum x1, other arithmetic, local(): output_grad = jnp.sum(lax.all_gather(grad_term, 'tile'), axis=0)  47 us
    all_gather x1, waiting for transfers between devices, local(): lax.all_gather(values, 'tile', axis=0, tiled=True).reshape(-1, HEADS, HD)  34.3 us
    dot_general x1, matrix products, local(): jnp.einsum('hqk,khd->hqd', weights.astype(jnp.bfloat16), value_heads, pre...  22.2 us
    dot_general x1, matrix products, local(): jnp.einsum('qhd,khd->hqk', query, key_heads, preferred_element_type=jnp.f...  22 us
    reduce_sum x1, other arithmetic, local(): total = jnp.sum(weights, axis=-1)  21.7 us
  transfers between devices with their start and end apart: 4, of which 4 were waited for; matrix products, arithmetic and copies ran while one was open for 7% of the time, Pallas kernels for 0%

profile of v1, /device:TPU:0, one launch (start us, length us, event | category | flops | bytes accessed | tf_op | source)
XLA Modules:
  0.0 988.2 jit_solution(14102967267242529243)
XLA Ops:
  7.2 0.9 fusion.77
  8.1 1.1 fusion.78
  9.3 0.7 pad_maximum_fusion.3
  10.0 1.3 fusion.68
  11.3 81.0 %all-gather.6.cloned.1.call-done = bf16[128,4,32,256]{3,2,1,0:T(8,128)(2,1)} async-done(((bf16[2,4,32,256]{3,2,1,0:T(8,128)(2,1)}), bf16[128,4,32,256]{3,2,1,0:T(8,128)(2,1)}) %all-gather.6.cloned.1.call-update) | async-done | bytes 8388624 | tf_op jit(solution)/shard_map/all_gather | solution.py:65
  92.3 8.5 concatenate.53
  100.8 1.5 gather_fusion.7
  102.3 1.5 gather_fusion.5
  103.8 1.5 gather_fusion.2
  105.3 1.5 gather_fusion
  106.8 4.0 gather_fusion.6
  110.7 4.0 gather_fusion.4
  114.7 4.0 gather_fusion.3
  118.6 4.0 gather_fusion.1
  122.7 1.2 pad_maximum_fusion.1
  124.0 1.7 pad_maximum_fusion
  125.7 0.8 fusion.75
  126.5 0.8 fusion.76
  127.3 0.5 copy-done.5
  127.7 0.4 fusion.32
  128.2 0.4 convolution_add_fusion.7
  128.6 0.4 convolution_add_fusion.6
  129.1 0.4 convolution_add_fusion.5
  129.5 0.4 convolution_add_fusion.4
  130.0 0.4 convolution_add_fusion.3
  130.4 0.4 convolution_add_fusion.2
  130.8 0.4 convolution_add_fusion.1
  131.3 0.9 fusion.13
  132.2 0.3 reshape_reshape.3
  132.5 0.4 copy.60
  132.9 0.8 reshape.58
  133.7 3.8 convolution_convert_fusion.3
  137.5 1.0 convolution_convert_fusion.1
  138.6 2.3 convolution_convert_fusion
  140.9 0.2 all-gather.12.cloned.1.call-start
  141.2 0.3 convolution_convert_fusion.2
  141.5 0.2 copy.52
  141.7 87.5 %all-gather.8.cloned.1.call-done = bf16[8192,768]{1,0:T(8,128)(2,1)} async-done(((bf16[128,768]{1,0:T(8,128)(2,1)}), bf16[8192,768]{1,0:T(8,128)(2,1)}) %all-gather.8.cloned.1.call-update) | async-done | bytes 12582928 | tf_op jit(solution)/shard_map/all_gather | solution.py:84
  229.2 15.8 %copy.53 = bf16[8192,768]{0,1:T(8,128)(2,1)} copy(bf16[8192,768]{1,0:T(8,128)(2,1)} %all-gather.8.cloned.1.call-done) | data formatting | bytes 25165824 | tf_op jit(solution)/shard_map/all_gather | solution.py:84
  245.0 22.0 %multiply_reduce_fusion = (f32[12,128]{1,0:T(8,128)S(1)}, f32[12,128,8192]{2,1,0:T(8,128)}) fusion(bf16[128,12,64]{0,2,1:T(8,128)(2,1)S(1)} %bitcast.107, bf16[8192,12,64]{0,2,1:T(8,128)(2,1)} %bitcast.93), kind=kOutput, calls=%fused_computation.9 | convolution fusion | flops 1635777024 | bytes 63117312 | tf_op jit(solution)/shard_map/qhd,khd->hqk/dot_general | solution.py:87
  267.0 21.7 %fusion = f32[12,128]{1,0:T(8,128)S(1)} fusion(f32[12,128,8192]{2,1,0:T(8,128)} %get-tuple-element.25, f32[12,128]{1,0:T(8,128)S(1)} %broadcast_maximum_fusion), kind=kLoop, calls=%fused_computation.10 | loop fusion | flops 37747200 | bytes 50343936 | tf_op jit(solution)/shard_map/reduce_sum | solution.py:91
  288.8 34.3 %all-gather.10.cloned.1.call-done = bf16[8192,768]{1,0:T(8,128)(2,1)} async-done(((bf16[128,768]{1,0:T(8,128)(2,1)}), bf16[8192,768]{1,0:T(8,128)(2,1)}) %all-gather.10.cloned.1.call-update) | async-done | bytes 12582928 | tf_op jit(solution)/shard_map/all_gather | solution.py:85
  323.1 15.8 %copy.54 = bf16[8192,768]{0,1:T(8,128)(2,1)} copy(bf16[8192,768]{1,0:T(8,128)(2,1)} %all-gather.10.cloned.1.call-done) | data formatting | bytes 25165824 | tf_op jit(solution)/shard_map/all_gather | solution.py:85
  338.8 22.2 %fusion.21 = bf16[128,12,64]{0,2,1:T(8,128)(2,1)S(1)} fusion(bf16[8192,12,64]{0,2,1:T(8,128)(2,1)} %bitcast.94, f32[12,128,8192]{2,1,0:T(8,128)} %get-tuple-element.25, f32[12,128]{1,0:T(8,128)S(1)} %broadcast_maximum_fusion, f32[128,12]{0,1:T(8,128)S(1)} %bitcast.110), kind=kOutput, calls=%fused_computation.42 | convolution fusion | flops 1648558080 | bytes 63123456 | tf_op jit(solution)/shard_map/hqk,khd->hqd/dot_general | solution.py:92
  361.1 1.9 fusion.79
  363.0 1.0 fusion.17
  364.0 570.6 %all-gather.12.cloned.1.call-done = f32[49152,768]{1,0:T(8,128)} async-done(((f32[768,768]{1,0:T(8,128)}), f32[49152,768]{1,0:T(8,128)}) %all-gather.12.cloned.1.call-update) | async-done | bytes 150994960 | tf_op jit(solution)/shard_map/all_gather | solution.py:107
  934.7 47.0 %reduce_sum.19 = f32[768,768]{1,0:T(8,128)} reduce(f32[64,768,768]{2,1,0:T(8,128)} %bitcast.37, f32[]{:T(128)} %constant.12.clone.1), dimensions={0}, to_apply=%region_2.0 | reduce | flops 37158912 | bytes 153354240 | tf_op jit(solution)/shard_map/reduce_sum | solution.py:107
  (30 shorter events, 0.4 us)
Async XLA Ops:
  7.2 130.4 %copy-start = (bf16[768,768]{1,0:T(8,128)(2,1)S(1)}, bf16[768,768]{1,0:T(8,128)(2,1)}, u32[]{:S(2)}) copy-start(bf16[768,768]{1,0:T(8,128)(2,1)} %param.14) | copy-start | bytes 3538948
  7.2 85.1 %all-gather.6.cloned.1.call-start = ((), (), s32[]{:S(2)}) async-start(), calls=%async_computation | async-start | bytes 8519680 | tf_op jit(solution)/shard_map/all_gather | solution.py:65
  10.0 219.2 %all-gather.8.cloned.1.call-start = ((), (), s32[]{:S(2)}) async-start(), calls=%async_computation.1 | async-start | bytes 12779520 | tf_op jit(solution)/shard_map/all_gather | solution.py:84
  11.3 111.5 %copy-start.2 = (bf16[2,32,32,256]{3,2,1,0:T(8,128)(2,1)S(1)}, bf16[2,32,32,256]{3,2,1,0:T(8,128)(2,1)}, u32[]{:S(2)}) copy-start(bf16[2,32,32,256]{3,2,1,0:T(8,128)(2,1)} %param.9) | copy-start | bytes 3145732
  126.5 1.3 copy-start.5
  137.5 3.6 copy-start.3
  138.6 184.5 %all-gather.10.cloned.1.call-start = ((), (), s32[]{:S(2)}) async-start(), calls=%async_computation.2 | async-start | bytes 12779520 | tf_op jit(solution)/shard_map/all_gather | solution.py:85
  140.9 793.7 %all-gather.12.cloned.1.call-start = ((), (), s32[]{:S(2)}) async-start(), calls=%async_computation.3 | async-start | bytes 153354240 | tf_op jit(solution)/shard_map/all_gather | solution.py:107
  338.8 22.2 %copy-start.6 = (bf16[128,768]{1,0:T(8,128)(2,1)S(1)}, bf16[128,768]{1,0:T(8,128)(2,1)}, u32[]{:S(2)}) copy-start(bf16[128,768]{1,0:T(8,128)(2,1)} %param.17) | copy-start | bytes 589828
  361.1 1.9 copy-start.4
  934.7 47.0 %copy-start.1 = (bf16[768,768]{1,0:T(8,128)(2,1)S(1)}, bf16[768,768]{1,0:T(8,128)(2,1)}, u32[]{:S(2)}) copy-start(bf16[768,768]{1,0:T(8,128)(2,1)} %param.14) | copy-start | bytes 3538948
Sparse Core Ops, SparseCore 0:
  11.4 80.8 all-gather.5
  138.7 90.4 all-gather.7
  232.5 90.5 all-gather.9
  363.1 571.5 all-gather.11
